TPU v7x, 512 devices: a whole 4x4x16 slice. The times are simulated.
512 devices in a mesh: gx: 4 (over x_lo, core), gy: 8 (over x_hi, y), gz: 16 (over z).
Axes of the slice: x: 4 (x_hi: 2, x_lo: 2; x = x_hi * 2 + x_lo), y: 4, z: 16, core: 2. Of those that a mesh axis runs over, the one named last changes fastest.
Arguments:
- density: float32 [128, 256, 2048], P('gz', 'gx', 'gy'), may hold values from 0.2 to 2
- bins: int32 [128, 256, 2048], P('gz', 'gx', 'gy'), may hold values from 0 to 255
- colour_table: bfloat16 [3, 256], replicated, may hold values from 0.049804688 to 1
- opacity_table: bfloat16 [256], replicated, may hold values from 0.19921875 to 2.5
- order: int32 [4, 8, 16], P('gx', 'gy'), may hold values from 0 to 15, each once within a row
Outputs:
- image: float32 [4, 256, 2048], P(None, ('gx', 'gz'), 'gy')
Inputs may be any that keep to these rules, and one draw needn't show every extreme that they name: For each column block and row block, order holds each brick rank 0 to 15 once.
All inputs are finite; a program needn't handle non-finite values.
Results may differ from a plain program's by a relative error of at most 0.0003.
Values sent between devices are 32-bit elements; how exact they have to be, the bound alone decides.
A program may use at most 64 MiB of HBM per device.

v0:
```python
import jax
import jax.numpy as jnp
from jax import lax
from jax.sharding import PartitionSpec as P


def padded_2(x, sides, width):
    for axis, dim in sides:
        devices, length = (lax.axis_size(axis), x.shape[dim])
        up = [(i, (i + 1) % devices) for i in range(devices - 1)]
        down = [(j, i) for i, j in up]
        last = lax.slice_in_dim(x, length - width, length, axis=dim)
        first = lax.slice_in_dim(x, 0, width, axis=dim)
        before = lax.ppermute(last, axis, up)
        after = lax.ppermute(first, axis, down)
        x = jnp.concatenate([before, x, after], axis=dim)
    return x


def local(density, bins, colour_table, opacity_table, order):
    ranks = order.reshape(-1)
    depth_cells, column_cells, row_cells = density.shape
    bricks = lax.axis_size("gz")
    total_depth = depth_cells * bricks
    table_size = colour_table.shape[1]
    padded = padded_2(density, (("gx", 1), ("gy", 2), ("gz", 0)), 1)
    slope_depth = (padded[2:, 1:-1, 1:-1] - padded[:-2, 1:-1, 1:-1]) * 0.5
    slope_column = (padded[1:-1, 2:, 1:-1] - padded[1:-1, :-2, 1:-1]) * 0.5
    slope_row = (padded[1:-1, 1:-1, 2:] - padded[1:-1, 1:-1, :-2]) * 0.5
    facing = 0.64 * slope_depth + 0.48 * slope_column + 0.6 * slope_row
    length = jnp.sqrt(
        slope_depth * slope_depth + slope_column * slope_column + slope_row * slope_row + 1.0
    )
    shade = 0.25 + 0.75 * jnp.abs(facing) / length
    table_four = jnp.concatenate([colour_table, opacity_table[None, :]], axis=0)
    plane_cells = column_cells * row_cells
    flat_bins = bins.reshape(2 * depth_cells, plane_cells // 2)
    entries = jnp.arange(table_size, dtype=jnp.int32)

    def lookup(block):
        onehot = (block[None, :] == entries[:, None]).astype(jnp.bfloat16)
        return jnp.dot(table_four, onehot, preferred_element_type=jnp.float32)

    looked = lax.map(lookup, flat_bins)
    looked = jnp.transpose(looked, (1, 0, 2)).reshape(4, depth_cells, column_cells, row_cells)
    sigma = looked[3] * density * (3.0 / total_depth)
    alpha = 1.0 - jnp.exp(-sigma)
    excl = jnp.cumsum(sigma, axis=0) - sigma
    weight = jnp.exp(-excl) * alpha * shade
    colour_local = jnp.sum(weight[None] * looked[:3], axis=1)
    depth_local = jnp.sum(sigma, axis=0)
    tile_rows = column_cells // bricks
    all_depth = lax.all_gather(depth_local[None], "gz", axis=0, tiled=True)
    mine = ranks[lax.axis_index("gz")]
    earlier = (ranks < mine).astype(jnp.float32)
    prefix = jnp.sum(earlier[:, None, None] * all_depth, axis=0)
    attenuated = jnp.exp(-prefix)[None] * colour_local
    colour_tile = lax.psum_scatter(attenuated, "gz", scatter_dimension=1, tiled=True)
    total = jnp.sum(all_depth, axis=0)
    total_tile = lax.dynamic_slice_in_dim(total, lax.axis_index("gz") * tile_rows, tile_rows, 0)
    opacity_tile = 1.0 - jnp.exp(-total_tile)
    return jnp.concatenate([colour_tile, opacity_tile[None]], axis=0)


def solution(mesh):
    return jax.shard_map(
        local,
        mesh=mesh,
        in_specs=(P("gz", "gx", "gy"), P("gz", "gx", "gy"), P(), P(), P("gx", "gy", None)),
        out_specs=P(None, ("gx", "gz"), "gy"),
        check_vma=False,
    )
```

profile of v0, /device:TPU:6, one launch (start us, length us, event | category | flops | bytes accessed | tf_op | source)
XLA Modules:
  0.0 255.1 jit_solution(7183533164202776697)
XLA Ops:
  9.0 22.4 %while.11 = (s32[]{:T(128)}, f32[16,4,8192]{2,1,0:T(4,128)S(1)}, s32[16,8192]{1,0:T(8,128)S(1)}, bf16[4,256]{1,0:T(4,128)(2,1)S(1)}, s32[]{:T(128)}) while((s32[]{:T(128)}, f32[16,4,8192]{2,1,0:T(4,128)S(1)}, s32[16,8192]{1,0:T(8,128)S(1)}, bf16[4,256]{1,0:T(4,128)(2,1)S(1)}, s32[]{:T(128)}) %tuple.25), condition=%wide.region_1.2_spmd.clone, body=%wide.region_0.1_spmd.clone.sunk | while | flops 18874368 | bytes 231501 | solution.py:44
  9.1 1.4 fusion.21
  10.5 1.4 fusion.21
  11.9 1.4 fusion.21
  13.3 1.4 fusion.21
  14.7 1.4 fusion.21
  16.1 1.4 fusion.21
  17.5 1.4 fusion.21
  18.9 1.4 fusion.21
  31.5 2.3 slice_reduce_fusion
  35.7 2.2 collective-permute-start.1
  37.9 2.1 collective-permute-start
  40.0 2.8 %collective-permute-done = f32[8,1,256]{2,1,0:T(1,128)S(1)} collective-permute-done((f32[8,1,256]{2,1,0:T(1,128)S(1)}, f32[8,1,256]{2,1,0:T(1,128)S(1)}, u32[]{:S(2)}, u32[]{:S(2)}) %collective-permute-start) | collective-permute-done | bytes 8224 | tf_op jit(solution)/shard_map/ppermute | solution.py:14
  43.8 3.5 %collective-permute-start.2 = (f32[8,66,1]{2,1,0:T(8,128)}, f32[8,66,1]{2,1,0:T(8,128)S(1)}, u32[]{:S(2)}, u32[]{:S(2)}) collective-permute-start(f32[8,66,1]{2,1,0:T(8,128)} %get-tuple-element.56), channel_id=1, source_target_pairs={{0,16},{16,32},{32,48},{48,64},{64,80},{80,96},{96,112},{1,17},{17... | collective-permute-start | bytes 6344 | tf_op jit(solution)/shard_map/ppermute | solution.py:14
  47.3 6.0 %collective-permute-start.3 = (f32[8,66,1]{2,1,0:T(8,128)}, f32[8,66,1]{2,1,0:T(8,128)}, u32[]{:S(2)}, u32[]{:S(2)}) collective-permute-start(f32[8,66,1]{2,1,0:T(8,128)} %get-tuple-element.55), channel_id=1, source_target_pairs={{16,0},{32,16},{48,32},{64,48},{80,64},{96,80},{112,96},{17,1},{33... | collective-permute-start | bytes 6344 | tf_op jit(solution)/shard_map/ppermute | solution.py:15
  53.9 2.9 %collective-permute-done.2 = f32[8,66,1]{2,1,0:T(8,128)S(1)} collective-permute-done((f32[8,66,1]{2,1,0:T(8,128)}, f32[8,66,1]{2,1,0:T(8,128)S(1)}, u32[]{:S(2)}, u32[]{:S(2)}) %collective-permute-start.2) | collective-permute-done | bytes 2144 | tf_op jit(solution)/shard_map/ppermute | solution.py:14
  58.0 1.7 pad_maximum_fusion.23
  59.7 3.8 %collective-permute-start.5 = (f32[1,66,258]{2,1,0:T(8,128)}, f32[1,66,258]{2,1,0:T(8,128)S(1)}, u32[]{:S(2)}, u32[]{:S(2)}) collective-permute-start(f32[1,66,258]{2,1,0:T(8,128)} %get-tuple-element.54), channel_id=1, source_target_pairs={{0,1},{1,2},{2,3},{3,4},{4,5},{5,6},{6,7},{7,8},{8,9},{9,10},{10,1... | collective-permute-start | bytes 204344 | tf_op jit(solution)/shard_map/ppermute | solution.py:14
  66.1 2.1 copy.8
  68.1 1.5 slice.66
  70.5 1.9 fusion.7
  72.6 38.5 %all-gather.3.cloned.1.call-done = f32[1024,256]{1,0:T(8,128)} async-done(((f32[64,256]{1,0:T(8,128)}), f32[1024,256]{1,0:T(8,128)}) %all-gather.3.cloned.1.call-update) | async-done | bytes 1048592 | tf_op jit(solution)/shard_map/all_gather | solution.py:53
  111.1 1.4 multiply_reduce_fusion.1
  115.2 131.8 %all-reduce.3.cloned.1.call-done = f32[3,64,256]{2,1,0:T(8,128)} async-done(((f32[3,64,256]{2,1,0:T(8,128)}), f32[3,64,256]{2,1,0:T(8,128)}) %all-reduce.3.cloned.1.call-update) | async-done | bytes 196624
  (63 shorter events, 25.5 us)
Async XLA Ops:
  6.5 104.5 %all-gather.3.cloned.1.call-start = ((), (), s32[]{:S(2)}) async-start(), calls=%async_computation | async-start | bytes 1114112 | tf_op jit(solution)/shard_map/all_gather | solution.py:53
  31.5 3.4 %copy-start = (f32[8,64,256]{2,1,0:T(8,128)S(1)}, f32[8,64,256]{2,1,0:T(8,128)}, u32[]{:S(2)}) copy-start(f32[8,64,256]{2,1,0:T(8,128)} %param.7) | copy-start | bytes 1572868
  33.8 19.5 %copy-start.5 = (s32[1,1,16]{2,1,0:T(1,128)S(1)}, s32[1,1,16]{2,1,0:T(1,128)}, u32[]{:S(2)}) copy-start(s32[1,1,16]{2,1,0:T(1,128)} %param.11) | copy-start | bytes 196
  35.6 211.3 %all-reduce.3.cloned.1.call-start = ((), (), s32[]{:S(2)}) async-start(), calls=%async_computation.1 | async-start | bytes 393216
  35.7 4.3 %collective-permute-start.1 = (f32[8,1,256]{2,1,0:T(1,128)S(1)}, f32[8,1,256]{2,1,0:T(1,128)S(1)}, u32[]{:S(2)}, u32[]{:S(2)}) collective-permute-start(f32[8,1,256]{2,1,0:T(1,128)S(1)} %get-tuple-element.58), channel_id=1, source_target_pairs={{128,0},{256,128},{384,256},{129,1},{257,129},{385,257},{130,2},{2... | collective-permute-start | bytes 24584 | tf_op jit(solution)/shard_map/ppermute | solution.py:15
  37.9 5.0 %collective-permute-start = (f32[8,1,256]{2,1,0:T(1,128)S(1)}, f32[8,1,256]{2,1,0:T(1,128)S(1)}, u32[]{:S(2)}, u32[]{:S(2)}) collective-permute-start(f32[8,1,256]{2,1,0:T(1,128)S(1)} %get-tuple-element.57), channel_id=1, source_target_pairs={{0,128},{128,256},{256,384},{1,129},{129,257},{257,385},{2,130},{1... | collective-permute-start | bytes 24584 | tf_op jit(solution)/shard_map/ppermute | solution.py:14
  40.0 19.7 %copy-start.1 = (f32[8,1,256]{2,1,0:T(1,128)}, f32[8,1,256]{2,1,0:T(1,128)S(1)}, u32[]{:S(2)}) copy-start(f32[8,1,256]{2,1,0:T(1,128)S(1)} %collective-permute-done.1) | copy-start | bytes 24580
  42.8 16.9 %copy-start.3 = (f32[8,1,256]{2,1,0:T(1,128)}, f32[8,1,256]{2,1,0:T(1,128)S(1)}, u32[]{:S(2)}) copy-start(f32[8,1,256]{2,1,0:T(1,128)S(1)} %collective-permute-done) | copy-start | bytes 24580
  43.8 13.0 %collective-permute-start.2 = (f32[8,66,1]{2,1,0:T(8,128)}, f32[8,66,1]{2,1,0:T(8,128)S(1)}, u32[]{:S(2)}, u32[]{:S(2)}) collective-permute-start(f32[8,66,1]{2,1,0:T(8,128)} %get-tuple-element.56), channel_id=1, source_target_pairs={{0,16},{16,32},{32,48},{48,64},{64,80},{80,96},{96,112},{1,17},{17... | collective-permute-start | bytes 6344 | tf_op jit(solution)/shard_map/ppermute | solution.py:14
  47.3 10.8 %collective-permute-start.3 = (f32[8,66,1]{2,1,0:T(8,128)}, f32[8,66,1]{2,1,0:T(8,128)}, u32[]{:S(2)}, u32[]{:S(2)}) collective-permute-start(f32[8,66,1]{2,1,0:T(8,128)} %get-tuple-element.55), channel_id=1, source_target_pairs={{16,0},{32,16},{48,32},{64,48},{80,64},{96,80},{112,96},{17,1},{33... | collective-permute-start | bytes 6344 | tf_op jit(solution)/shard_map/ppermute | solution.py:15
  59.7 10.0 %collective-permute-start.5 = (f32[1,66,258]{2,1,0:T(8,128)}, f32[1,66,258]{2,1,0:T(8,128)S(1)}, u32[]{:S(2)}, u32[]{:S(2)}) collective-permute-start(f32[1,66,258]{2,1,0:T(8,128)} %get-tuple-element.54), channel_id=1, source_target_pairs={{0,1},{1,2},{2,3},{3,4},{4,5},{5,6},{6,7},{7,8},{8,9},{9,10},{10,1... | collective-permute-start | bytes 204344 | tf_op jit(solution)/shard_map/ppermute | solution.py:14
  63.5 7.0 %collective-permute-start.4 = (f32[1,66,258]{2,1,0:T(8,128)}, f32[1,66,258]{2,1,0:T(8,128)}, u32[]{:S(2)}, u32[]{:S(2)}) collective-permute-start(f32[1,66,258]{2,1,0:T(8,128)} %get-tuple-element.53), channel_id=1, source_target_pairs={{1,0},{2,1},{3,2},{4,3},{5,4},{6,5},{7,6},{8,7},{9,8},{10,9},{11,1... | collective-permute-start | bytes 204344 | tf_op jit(solution)/shard_map/ppermute | solution.py:15
  68.1 2.3 copy-start.2
  68.1 2.4 copy-start.4
Sparse Core Ops, SparseCore 0:
  35.7 75.2 all-gather.2
  113.4 133.4 all-reduce.2
where the time goes:
time: 256 us; the launch traced here: 255 us
  waiting for transfers between devices  178 us (70%)
  matrix products  21.9 us (9%)
  starting transfers between devices  18.9 us (7%)
  between operations  14.2 us (6%)
  local copies, waits for them, and re-layouts  12.8 us (5%)
  other arithmetic  9.13 us (4%)
    unnamed x3, waiting for transfers between devices  132 us
    all_gather x1, waiting for transfers between devices, local(): all_depth = lax.all_gather(depth_local[None], 'gz', axis=0, tiled=True)  38.5 us
    dot_general x16, matrix products, lookup(): return jnp.dot(table_four, onehot, preferred_element_type=jnp.float32)  21.9 us
    ppermute x3, starting transfers between devices, padded_2(): before = lax.ppermute(last, axis, up)  9.44 us
    ppermute x3, starting transfers between devices, padded_2(): after = lax.ppermute(first, axis, down)  9.44 us
    ppermute x3, waiting for transfers between devices, padded_2(): before = lax.ppermute(last, axis, up)  5.7 us
  transfers between devices with their start and end apart: 8, of which 6 were waited for; matrix products, arithmetic and copies ran while one was open for 4% of the time, Pallas kernels for 0%

commit v1 on v0

v1 whole, which is shorter than its diff:
```python
import functools
import math

import jax
import jax.numpy as jnp
from jax import lax
from jax.experimental import pallas as pl
from jax.experimental.pallas import tpu as pltpu
from jax.sharding import PartitionSpec as P

MESH = pl.DeviceIdType.MESH
LANES = 128
ROWS = 8
F32 = jnp.float32


def kernel(
    n_z,
    scale,
    dens_hbm,
    bins_hbm,
    ctab_ref,
    otab_ref,
    order_ref,
    out_ref,
    dens,
    bins,
    tabs,
    weight,
    edge,
    halo,
    send,
    recv,
    inv,
    load_sem,
    halo_send,
    halo_recv,
    tile_send,
    tile_recv,
    known,
):
    gx, gy, me = lax.axis_index("gx"), lax.axis_index("gy"), lax.axis_index("gz")
    n_x, n_y = lax.axis_size("gx"), lax.axis_size("gy")
    depth, _, height, _ = bins.shape
    blocks = height // ROWS

    def step(index, count, by):
        return lax.rem(index + (by + count), count)

    neighbours = [
        {"gx": step(gx, n_x, -1)},
        {"gx": step(gx, n_x, 1)},
        {"gy": step(gy, n_y, -1)},
        {"gy": step(gy, n_y, 1)},
        {"gz": step(me, n_z, -1)},
        {"gz": step(me, n_z, 1)},
    ]

    loads = []
    for half in range(2):
        lanes = pl.ds(half * LANES, LANES)
        loads.append(
            pltpu.make_async_copy(
                dens_hbm.at[:, :, lanes],
                dens.at[pl.ds(1, depth), half, pl.ds(ROWS, height), :],
                load_sem.at[half],
            )
        )
    for half in range(2):
        lanes = pl.ds(half * LANES, LANES)
        loads.append(
            pltpu.make_async_copy(
                bins_hbm.at[:, :, lanes], bins.at[:, half], load_sem.at[2 + half]
            )
        )
    for load in loads:
        load.start()

    barrier = pltpu.get_barrier_semaphore()
    for other in neighbours:
        pl.semaphore_signal(barrier, inc=1, device_id=other, device_id_type=MESH)

    table = jnp.concatenate(
        [ctab_ref[...].astype(F32), otab_ref[...].astype(F32) * scale], axis=0
    )
    for c in range(4):
        for half in range(2):
            row = table[c : c + 1, half * LANES : (half + 1) * LANES]
            tabs[c, half] = jnp.broadcast_to(row, (ROWS, LANES))

    pl.semaphore_wait(barrier, len(neighbours))

    def greet(level):
        for sign in (-1, 1):
            pl.semaphore_signal(
                known.at[level],
                inc=1,
                device_id={"gz": step(me, n_z, sign * (1 << level))},
                device_id_type=MESH,
            )

    greet(0)
    loads[0].wait()
    loads[1].wait()

    def remote(src, dst, index, other):
        return pltpu.make_async_remote_copy(
            src_ref=src,
            dst_ref=dst,
            send_sem=halo_send.at[index],
            recv_sem=halo_recv.at[index],
            device_id=other,
            device_id_type=MESH,
        )

    own_rows = pl.ds(ROWS, height)
    own_planes = pl.ds(1, depth)
    z_up = remote(
        dens.at[depth, :, own_rows, :], dens.at[0, :, own_rows, :], 0, neighbours[5]
    )
    z_down = remote(
        dens.at[1, :, own_rows, :],
        dens.at[depth + 1, :, own_rows, :],
        1,
        neighbours[4],
    )
    x_up = remote(
        dens.at[own_planes, :, pl.ds(height, ROWS), :],
        dens.at[own_planes, :, pl.ds(0, ROWS), :],
        2,
        neighbours[1],
    )
    x_down = remote(
        dens.at[own_planes, :, pl.ds(ROWS, ROWS), :],
        dens.at[own_planes, :, pl.ds(height + ROWS, ROWS), :],
        3,
        neighbours[0],
    )
    copies = [z_up, z_down, x_up, x_down]
    for copy in copies:
        copy.start()

    lane = lax.broadcasted_iota(jnp.int32, (ROWS, LANES), 1)
    sub = lax.broadcasted_iota(jnp.int32, (ROWS, LANES), 0)

    first = jnp.zeros((ROWS, LANES), F32)
    last = jnp.zeros((ROWS, LANES), F32)
    for z in range(depth):
        for b in range(blocks):
            k = z * blocks + b
            rows = pl.ds(ROWS + b * ROWS, ROWS)
            first = jnp.where(
                lane == k, jnp.broadcast_to(dens[z + 1, 0, rows, 0:1], first.shape), first
            )
            last = jnp.where(
                lane == k,
                jnp.broadcast_to(dens[z + 1, 1, rows, LANES - 1 : LANES], last.shape),
                last,
            )
    edge[0] = first
    edge[1] = last
    y_up = remote(edge.at[1], halo.at[0], 4, neighbours[3])
    y_down = remote(edge.at[0], halo.at[1], 5, neighbours[2])
    y_up.start()
    y_down.start()
    copies += [y_up, y_down]

    pl.semaphore_wait(known.at[0], 2)
    greet(1)

    def split(block, channel, low, high):
        send[2 * block, channel] = jnp.where(sub < 4, low, pltpu.roll(high, 4, 0))
        send[2 * block + 1, channel] = jnp.where(sub < 4, pltpu.roll(low, 4, 0), high)

    def looked(c, index, upper):
        return jnp.where(
            upper,
            jnp.take_along_axis(tabs[c, 1], index, axis=1, mode="promise_in_bounds"),
            jnp.take_along_axis(tabs[c, 0], index, axis=1, mode="promise_in_bounds"),
        )

    loads[2].wait()
    loads[3].wait()

    def optical(block, carry):
        rows = pl.ds(pl.multiple_of(block * ROWS, ROWS), ROWS)
        padded = pl.ds(pl.multiple_of(block * ROWS + ROWS, ROWS), ROWS)
        ends = []
        for half in range(2):
            total = jnp.zeros((ROWS, LANES), F32)
            before = jnp.ones((ROWS, LANES), F32)
            for z in range(depth):
                bin_ = bins[z, half, rows, :]
                sigma = looked(3, bin_ & (LANES - 1), bin_ >= LANES)
                total = total + sigma * dens[z + 1, half, padded, :]
                after = jnp.exp2(total)
                weight[z, half, rows, :] = before - after
                before = after
            ends.append(total)
        split(block, 3, *ends)
        return carry

    lax.fori_loop(0, blocks, optical, 0)

    pl.semaphore_wait(known.at[1], 2)
    greet(2)

    def place(rank, carry):
        slot = jnp.int32(0)
        for b in range(n_z):
            here = lax.rem(me + (n_z - b), n_z)
            slot = jnp.where(order_ref[0, 0, b] == rank, here, slot)
        inv[rank] = slot
        return carry

    lax.fori_loop(0, n_z, place, 0)

    for copy in copies:
        copy.wait_recv()

    blank = jnp.zeros((ROWS, LANES), F32)

    @pl.when(gx == 0)
    def _():
        for z in range(depth):
            for half in range(2):
                dens[z + 1, half, pl.ds(0, ROWS), :] = blank

    @pl.when(gx == n_x - 1)
    def _():
        for z in range(depth):
            for half in range(2):
                dens[z + 1, half, pl.ds(height + ROWS, ROWS), :] = blank

    @pl.when(gy == 0)
    def _():
        halo[0] = blank

    @pl.when(gy == n_y - 1)
    def _():
        halo[1] = blank

    @pl.when(me == 0)
    def _():
        for half in range(2):
            dens[0, half, own_rows, :] = jnp.zeros((height, LANES), F32)

    @pl.when(me == n_z - 1)
    def _():
        for half in range(2):
            dens[depth + 1, half, own_rows, :] = jnp.zeros((height, LANES), F32)

    def tile(by):
        other = step(me, n_z, by)
        slot = by % n_z
        return pltpu.make_async_remote_copy(
            src_ref=send.at[other],
            dst_ref=recv.at[slot],
            send_sem=tile_send.at[slot],
            recv_sem=tile_recv.at[slot],
            device_id={"gz": other},
            device_id_type=MESH,
        )

    def colours(k, carry):
        away = lax.div(k + 1, 2)
        away = jnp.where(lax.rem(k, 2) == 1, away, blocks - away)
        block = lax.rem(lax.div(me, 2) + away, blocks)
        rows = pl.ds(pl.multiple_of(block * ROWS, ROWS), ROWS)
        base = block * ROWS
        here = pl.ds(pl.multiple_of(base + ROWS, ROWS), ROWS)
        sums = [[jnp.zeros((ROWS, LANES), F32) for _ in range(2)] for _ in range(3)]
        for z in range(depth):
            low, high = dens[z + 1, 0, here, :], dens[z + 1, 1, here, :]
            column = z * blocks + block
            west = pltpu.roll(halo[0], LANES - column, 1)
            east = pltpu.roll(halo[1], LANES - 1 - column, 1)
            low_up, high_up = pltpu.roll(low, 1, 1), pltpu.roll(high, 1, 1)
            low_down = pltpu.roll(low, LANES - 1, 1)
            high_down = pltpu.roll(high, LANES - 1, 1)
            slopes_y = (
                jnp.where(lane == LANES - 1, high_down, low_down)
                - jnp.where(lane == 0, west, low_up),
                jnp.where(lane == LANES - 1, east, high_down)
                - jnp.where(lane == 0, low_up, high_up),
            )
            for half in range(2):
                slope_z = dens[z + 2, half, here, :] - dens[z, half, here, :]
                slope_x = (
                    dens[z + 1, half, pl.ds(base + ROWS + 1, ROWS), :]
                    - dens[z + 1, half, pl.ds(base + ROWS - 1, ROWS), :]
                )
                slope_y = slopes_y[half]
                facing = jnp.abs(0.48 * slope_z + 0.36 * slope_x + 0.45 * slope_y)
                square = (
                    slope_z * slope_z + slope_x * slope_x + slope_y * slope_y + 4.0
                )
                shade = 0.25 + facing * lax.rsqrt(square)
                shaded = weight[z, half, rows, :] * shade
                bin_ = bins[z, half, rows, :]
                index, upper = bin_ & (LANES - 1), bin_ >= LANES
                for c in range(3):
                    sums[c][half] = sums[c][half] + shaded * looked(c, index, upper)
        for c in range(3):
            split(block, c, *sums[c])

        @pl.when(k == 2)
        def _():
            for by in (1, -1, 2, -2):
                tile(by).start()

        @pl.when(k == 4)
        def _():
            for by in (3, -3, 4, -4):
                tile(by).start()

        return carry

    lax.fori_loop(0, blocks, colours, 0)

    pl.semaphore_wait(known.at[2], 2)
    for by in (8, 7, -7, 6, -6, 5, -5):
        tile(by).start()

    recv[0] = send[me]
    for by in (1, -1, 2, -2, 3, -3, 4, -4, 5, -5, 6, -6, 7, -7, 8):
        tile(by).wait_recv()

    ahead = jnp.zeros((ROWS, LANES), F32)
    image = [jnp.zeros((ROWS, LANES), F32) for _ in range(3)]
    for rank in range(n_z):
        slot = inv[rank]
        through = jnp.exp2(ahead)
        for c in range(3):
            image[c] = image[c] + through * recv[slot, c]
        ahead = ahead + recv[slot, 3]
    image.append(1.0 - jnp.exp2(ahead))
    for c in range(4):
        out_ref[c, :, 0:LANES] = image[c][0:4, :]
        out_ref[c, :, LANES : 2 * LANES] = image[c][4:8, :]

    for copy in copies:
        copy.wait_send()
    for by in (1, -1, 2, -2, 3, -3, 4, -4, 5, -5, 6, -6, 7, -7, 8):
        tile(by).wait_send()


def local(density, bins, colour_table, opacity_table, order):
    depth, height, width = density.shape
    n_z = lax.axis_size("gz")
    scale = -3.0 / (depth * n_z) * math.log2(math.e)
    vmem = pl.BlockSpec(memory_space=pltpu.VMEM)
    anywhere = pl.BlockSpec(memory_space=pl.ANY)
    return pl.pallas_call(
        functools.partial(kernel, n_z, scale),
        out_shape=jax.ShapeDtypeStruct((4, height // n_z, width), F32),
        in_specs=[
            anywhere,
            anywhere,
            vmem,
            vmem,
            pl.BlockSpec(memory_space=pltpu.SMEM),
        ],
        out_specs=vmem,
        scratch_shapes=[
            pltpu.VMEM((depth + 2, 2, height + 2 * ROWS, LANES), F32),
            pltpu.VMEM((depth, 2, height, LANES), jnp.int32),
            pltpu.VMEM((4, 2, ROWS, LANES), F32),
            pltpu.VMEM((depth, 2, height, LANES), F32),
            pltpu.VMEM((2, ROWS, LANES), F32),
            pltpu.VMEM((2, ROWS, LANES), F32),
            pltpu.VMEM((n_z, 4, ROWS, LANES), F32),
            pltpu.VMEM((n_z, 4, ROWS, LANES), F32),
            pltpu.SMEM((n_z,), jnp.int32),
            pltpu.SemaphoreType.DMA((4,)),
            pltpu.SemaphoreType.DMA((6,)),
            pltpu.SemaphoreType.DMA((6,)),
            pltpu.SemaphoreType.DMA((n_z,)),
            pltpu.SemaphoreType.DMA((n_z,)),
            pltpu.SemaphoreType.REGULAR((3,)),
        ],
        compiler_params=pltpu.CompilerParams(collective_id=0, has_side_effects=True),
    )(density, bins, colour_table, opacity_table.reshape(1, -1), order)


def solution(mesh):
    return jax.shard_map(
        local,
        mesh=mesh,
        in_specs=(
            P("gz", "gx", "gy"),
            P("gz", "gx", "gy"),
            P(),
            P(),
            P("gx", "gy", None),
        ),
        out_specs=P(None, ("gx", "gz"), "gy"),
        check_vma=False,
    )
```

time: 256 us -> 37.8 us (0.15)
  the two profiles are of different devices: /device:TPU:6 before, /device:TPU:4 now
where the time goes in v1:
time: 37.8 us; the launch traced here: 37.5 us
  Pallas kernels  35 us (93%)
  local copies, waits for them, and re-layouts  2.54 us (7%)
    pallas_call x1, Pallas kernels, local(): pl.pallas_call(functools.partial(kernel, n_z, scale), out_shape=jax.Shape...  35 us
    unnamed x1, local copies, waits for them, and re-layouts  1.32 us
    reshape x1, local copies, waits for them, and re-layouts, local(): opacity_table.reshape(1, -1)  1.22 us

profile of v1, /device:TPU:4, one launch (start us, length us, event | category | flops | bytes accessed | tf_op | source)
XLA Modules:
  0.0 37.5 jit_solution(6436793180847135211)
XLA Ops:
  0.0 1.2 %reshape.3.otab_ref = bf16[1,256]{1,0:T(2,128)(2,1)} reshape(bf16[256]{0:T(256)(128)(2,1)} %param.8) | data formatting | bytes 1024 | tf_op jit(solution)/shard_map/reshape | solution.py:383
  1.2 35.0 %shard_map.55 = f32[4,4,256]{2,1,0:T(4,128)} custom-call(f32[8,64,256]{2,1,0:T(8,128)} %dens_hbm.1, s32[8,64,256]{2,1,0:T(8,128)} %bins_hbm.1, bf16[3,256]{1,0:T(4,128)(2,1)} %ctab_ref.1, bf16[1,256]{1,0:T(2,128)(2,1)} %reshape.3.otab_ref, s32[1,1,16]{2,1,0:T(1,128)} %order_ref.1), custom_call_target="tpu_custom_call" | custom-call | tf_op jit(solution)/shard_map/pallas_call | solution.py:354
  36.2 1.3 %copy.7 = f32[4,4,256]{2,1,0:T(4,128)} copy(f32[4,4,256]{2,1,0:T(4,128)} %shard_map.55) | data formatting | bytes 32768

commit v2 on v1

--- a/solution.py
+++ b/solution.py
@@ -19,12 +19,15 @@
     scale,
     dens_hbm,
     bins_hbm,
+    ctab_hbm,
+    otab_hbm,
+    order_hbm,
+    out_ref,
+    dens,
+    bins,
     ctab_ref,
     otab_ref,
     order_ref,
-    out_ref,
-    dens,
-    bins,
     tabs,
     weight,
     edge,
@@ -35,9 +38,10 @@
     load_sem,
     halo_send,
     halo_recv,
-    tile_send,
-    tile_recv,
-    known,
+    depth_send,
+    depth_recv,
+    colour_send,
+    colour_recv,
 ):
     gx, gy, me = lax.axis_index("gx"), lax.axis_index("gy"), lax.axis_index("gz")
     n_x, n_y = lax.axis_size("gx"), lax.axis_size("gy")
@@ -52,9 +56,23 @@
         {"gx": step(gx, n_x, 1)},
         {"gy": step(gy, n_y, -1)},
         {"gy": step(gy, n_y, 1)},
-        {"gz": step(me, n_z, -1)},
-        {"gz": step(me, n_z, 1)},
     ]
+    below, above = {"gz": step(me, n_z, -1)}, {"gz": step(me, n_z, 1)}
+
+    barrier = pltpu.get_barrier_semaphore()
+    for other in neighbours:
+        pl.semaphore_signal(barrier, inc=1, device_id=other, device_id_type=MESH)
+
+    def greet(by, carry):
+        pl.semaphore_signal(
+            barrier,
+            inc=1,
+            device_id={"gz": lax.rem(me + by, n_z)},
+            device_id_type=MESH,
+        )
+        return carry
+
+    lax.fori_loop(1, n_z, greet, 0)
 
     loads = []
     for half in range(2):
@@ -73,72 +91,25 @@
                 bins_hbm.at[:, :, lanes], bins.at[:, half], load_sem.at[2 + half]
             )
         )
+    for index, (src, dst) in enumerate(
+        ((ctab_hbm, ctab_ref), (otab_hbm, otab_ref), (order_hbm, order_ref))
+    ):
+        loads.append(pltpu.make_async_copy(src, dst, load_sem.at[4 + index]))
     for load in loads:
         load.start()
-
-    barrier = pltpu.get_barrier_semaphore()
-    for other in neighbours:
-        pl.semaphore_signal(barrier, inc=1, device_id=other, device_id_type=MESH)
+    loads[4].wait()
+    loads[5].wait()
 
     table = jnp.concatenate(
-        [ctab_ref[...].astype(F32), otab_ref[...].astype(F32) * scale], axis=0
+        [ctab_ref[...].astype(F32), otab_ref[...].astype(F32).reshape(1, -1) * scale], axis=0
     )
     for c in range(4):
         for half in range(2):
             row = table[c : c + 1, half * LANES : (half + 1) * LANES]
             tabs[c, half] = jnp.broadcast_to(row, (ROWS, LANES))
 
-    pl.semaphore_wait(barrier, len(neighbours))
-
-    def greet(level):
-        for sign in (-1, 1):
-            pl.semaphore_signal(
-                known.at[level],
-                inc=1,
-                device_id={"gz": step(me, n_z, sign * (1 << level))},
-                device_id_type=MESH,
-            )
-
-    greet(0)
     loads[0].wait()
     loads[1].wait()
-
-    def remote(src, dst, index, other):
-        return pltpu.make_async_remote_copy(
-            src_ref=src,
-            dst_ref=dst,
-            send_sem=halo_send.at[index],
-            recv_sem=halo_recv.at[index],
-            device_id=other,
-            device_id_type=MESH,
-        )
-
-    own_rows = pl.ds(ROWS, height)
-    own_planes = pl.ds(1, depth)
-    z_up = remote(
-        dens.at[depth, :, own_rows, :], dens.at[0, :, own_rows, :], 0, neighbours[5]
-    )
-    z_down = remote(
-        dens.at[1, :, own_rows, :],
-        dens.at[depth + 1, :, own_rows, :],
-        1,
-        neighbours[4],
-    )
-    x_up = remote(
-        dens.at[own_planes, :, pl.ds(height, ROWS), :],
-        dens.at[own_planes, :, pl.ds(0, ROWS), :],
-        2,
-        neighbours[1],
-    )
-    x_down = remote(
-        dens.at[own_planes, :, pl.ds(ROWS, ROWS), :],
-        dens.at[own_planes, :, pl.ds(height + ROWS, ROWS), :],
-        3,
-        neighbours[0],
-    )
-    copies = [z_up, z_down, x_up, x_down]
-    for copy in copies:
-        copy.start()
 
     lane = lax.broadcasted_iota(jnp.int32, (ROWS, LANES), 1)
     sub = lax.broadcasted_iota(jnp.int32, (ROWS, LANES), 0)
@@ -159,15 +130,6 @@
             )
     edge[0] = first
     edge[1] = last
-    y_up = remote(edge.at[1], halo.at[0], 4, neighbours[3])
-    y_down = remote(edge.at[0], halo.at[1], 5, neighbours[2])
-    y_up.start()
-    y_down.start()
-    copies += [y_up, y_down]
-
-    pl.semaphore_wait(known.at[0], 2)
-    greet(1)
-
     def split(block, channel, low, high):
         send[2 * block, channel] = jnp.where(sub < 4, low, pltpu.roll(high, 4, 0))
         send[2 * block + 1, channel] = jnp.where(sub < 4, pltpu.roll(low, 4, 0), high)
@@ -202,8 +164,75 @@
 
     lax.fori_loop(0, blocks, optical, 0)
 
-    pl.semaphore_wait(known.at[1], 2)
-    greet(2)
+    def depth_to(other):
+        slot = lax.rem(other - me + n_z, n_z)
+        return pltpu.make_async_remote_copy(
+            src_ref=send.at[other, 3],
+            dst_ref=recv.at[slot, 3],
+            send_sem=depth_send.at[slot],
+            recv_sem=depth_recv.at[slot],
+            device_id={"gz": other},
+            device_id_type=MESH,
+        )
+
+    def colour_to(other):
+        slot = lax.rem(other - me + n_z, n_z)
+        return pltpu.make_async_remote_copy(
+            src_ref=send.at[other, pl.ds(0, 3)],
+            dst_ref=recv.at[slot, pl.ds(0, 3)],
+            send_sem=colour_send.at[slot],
+            recv_sem=colour_recv.at[slot],
+            device_id={"gz": other},
+            device_id_type=MESH,
+        )
+
+    def remote(src, dst, index, other):
+        return pltpu.make_async_remote_copy(
+            src_ref=src,
+            dst_ref=dst,
+            send_sem=halo_send.at[index],
+            recv_sem=halo_recv.at[index],
+            device_id=other,
+            device_id_type=MESH,
+        )
+
+    own_rows = pl.ds(ROWS, height)
+    own_planes = pl.ds(1, depth)
+    z_up = remote(
+        dens.at[depth, :, own_rows, :], dens.at[0, :, own_rows, :], 0, above
+    )
+    z_down = remote(
+        dens.at[1, :, own_rows, :],
+        dens.at[depth + 1, :, own_rows, :],
+        1,
+        below,
+    )
+    x_up = remote(
+        dens.at[own_planes, :, pl.ds(height, ROWS), :],
+        dens.at[own_planes, :, pl.ds(0, ROWS), :],
+        2,
+        neighbours[1],
+    )
+    x_down = remote(
+        dens.at[own_planes, :, pl.ds(ROWS, ROWS), :],
+        dens.at[own_planes, :, pl.ds(height + ROWS, ROWS), :],
+        3,
+        neighbours[0],
+    )
+
+    y_up = remote(edge.at[1], halo.at[0], 4, neighbours[3])
+    y_down = remote(edge.at[0], halo.at[1], 5, neighbours[2])
+    pl.semaphore_wait(barrier, len(neighbours) + n_z - 1)
+    copies = [z_up, z_down, y_up, y_down, x_up, x_down]
+    for copy in copies:
+        copy.start()
+
+    def send_depth(by, carry):
+        depth_to(lax.rem(me + by, n_z)).start()
+        return carry
+
+    lax.fori_loop(1, n_z, send_depth, 0)
+    loads[6].wait()
 
     def place(rank, carry):
         slot = jnp.int32(0)
@@ -250,22 +279,8 @@
         for half in range(2):
             dens[depth + 1, half, own_rows, :] = jnp.zeros((height, LANES), F32)
 
-    def tile(by):
-        other = step(me, n_z, by)
-        slot = by % n_z
-        return pltpu.make_async_remote_copy(
-            src_ref=send.at[other],
-            dst_ref=recv.at[slot],
-            send_sem=tile_send.at[slot],
-            recv_sem=tile_recv.at[slot],
-            device_id={"gz": other},
-            device_id_type=MESH,
-        )
-
     def colours(k, carry):
-        away = lax.div(k + 1, 2)
-        away = jnp.where(lax.rem(k, 2) == 1, away, blocks - away)
-        block = lax.rem(lax.div(me, 2) + away, blocks)
+        block = k
         rows = pl.ds(pl.multiple_of(block * ROWS, ROWS), ROWS)
         base = block * ROWS
         here = pl.ds(pl.multiple_of(base + ROWS, ROWS), ROWS)
@@ -304,27 +319,25 @@
         for c in range(3):
             split(block, c, *sums[c])
 
-        @pl.when(k == 2)
-        def _():
-            for by in (1, -1, 2, -2):
-                tile(by).start()
-
-        @pl.when(k == 4)
-        def _():
-            for by in (3, -3, 4, -4):
-                tile(by).start()
+        for other in (2 * block, 2 * block + 1):
+
+            @pl.when(other != me)
+            def _():
+                colour_to(other).start()
 
         return carry
 
     lax.fori_loop(0, blocks, colours, 0)
 
-    pl.semaphore_wait(known.at[2], 2)
-    for by in (8, 7, -7, 6, -6, 5, -5):
-        tile(by).start()
-
     recv[0] = send[me]
-    for by in (1, -1, 2, -2, 3, -3, 4, -4, 5, -5, 6, -6, 7, -7, 8):
-        tile(by).wait_recv()
+
+    def arrive(by, carry):
+        other = lax.rem(me + by, n_z)
+        depth_to(other).wait_recv()
+        colour_to(other).wait_recv()
+        return carry
+
+    lax.fori_loop(1, n_z, arrive, 0)
 
     ahead = jnp.zeros((ROWS, LANES), F32)
     image = [jnp.zeros((ROWS, LANES), F32) for _ in range(3)]
@@ -341,8 +354,14 @@
 
     for copy in copies:
         copy.wait_send()
-    for by in (1, -1, 2, -2, 3, -3, 4, -4, 5, -5, 6, -6, 7, -7, 8):
-        tile(by).wait_send()
+
+    def leave(by, carry):
+        other = lax.rem(me + by, n_z)
+        depth_to(other).wait_send()
+        colour_to(other).wait_send()
+        return carry
+
+    lax.fori_loop(1, n_z, leave, 0)
 
 
 def local(density, bins, colour_table, opacity_table, order):
@@ -354,17 +373,14 @@
     return pl.pallas_call(
         functools.partial(kernel, n_z, scale),
         out_shape=jax.ShapeDtypeStruct((4, height // n_z, width), F32),
-        in_specs=[
-            anywhere,
-            anywhere,
-            vmem,
-            vmem,
-            pl.BlockSpec(memory_space=pltpu.SMEM),
-        ],
+        in_specs=[anywhere] * 5,
         out_specs=vmem,
         scratch_shapes=[
             pltpu.VMEM((depth + 2, 2, height + 2 * ROWS, LANES), F32),
             pltpu.VMEM((depth, 2, height, LANES), jnp.int32),
+            pltpu.VMEM(colour_table.shape, colour_table.dtype),
+            pltpu.VMEM(opacity_table.shape, opacity_table.dtype),
+            pltpu.SMEM(order.shape, order.dtype),
             pltpu.VMEM((4, 2, ROWS, LANES), F32),
             pltpu.VMEM((depth, 2, height, LANES), F32),
             pltpu.VMEM((2, ROWS, LANES), F32),
@@ -372,15 +388,16 @@
             pltpu.VMEM((n_z, 4, ROWS, LANES), F32),
             pltpu.VMEM((n_z, 4, ROWS, LANES), F32),
             pltpu.SMEM((n_z,), jnp.int32),
-            pltpu.SemaphoreType.DMA((4,)),
+            pltpu.SemaphoreType.DMA((7,)),
             pltpu.SemaphoreType.DMA((6,)),
             pltpu.SemaphoreType.DMA((6,)),
             pltpu.SemaphoreType.DMA((n_z,)),
             pltpu.SemaphoreType.DMA((n_z,)),
-            pltpu.SemaphoreType.REGULAR((3,)),
+            pltpu.SemaphoreType.DMA((n_z,)),
+            pltpu.SemaphoreType.DMA((n_z,)),
         ],
         compiler_params=pltpu.CompilerParams(collective_id=0, has_side_effects=True),
-    )(density, bins, colour_table, opacity_table.reshape(1, -1), order)
+    )(density, bins, colour_table, opacity_table, order)
 
 
 def solution(mesh):

time: 37.8 us -> 32 us (0.85)
  the two profiles are of different devices: /device:TPU:4 before, /device:TPU:2 now
where the time goes in v2:
time: 32 us; the launch traced here: 31.9 us
  Pallas kernels  30.5 us (95%)
  local copies, waits for them, and re-layouts  1.32 us (4%)
    pallas_call x1, Pallas kernels, local(): pl.pallas_call(functools.partial(kernel, n_z, scale), out_shape=jax.Shape...  30.5 us
    unnamed x1, local copies, waits for them, and re-layouts  1.32 us

profile of v2, /device:TPU:2, one launch (start us, length us, event | category | flops | bytes accessed | tf_op | source)
XLA Modules:
  0.0 31.9 jit_solution(14760434654783504296)
XLA Ops:
  0.0 30.5 %shard_map.55 = f32[4,4,256]{2,1,0:T(4,128)} custom-call(f32[8,64,256]{2,1,0:T(8,128)} %dens_hbm.1, s32[8,64,256]{2,1,0:T(8,128)} %bins_hbm.1, bf16[3,256]{1,0:T(4,128)(2,1)} %ctab_hbm.1, bf16[256]{0:T(256)(128)(2,1)} %otab_hbm.1, s32[1,1,16]{2,1,0:T(1,128)} %order_hbm.1), custom_call_target="tpu_custom_call" | custom-call | tf_op jit(solution)/shard_map/pallas_call | solution.py:373
  30.5 1.3 %copy.7 = f32[4,4,256]{2,1,0:T(4,128)} copy(f32[4,4,256]{2,1,0:T(4,128)} %shard_map.55) | data formatting | bytes 32768

commit v3 on v2

--- a/solution.py
+++ b/solution.py
@@ -11,6 +11,7 @@
 MESH = pl.DeviceIdType.MESH
 LANES = 128
 ROWS = 8
+PARTS = 4
 F32 = jnp.float32
 
 
@@ -32,6 +33,8 @@
     weight,
     edge,
     halo,
+    rim,
+    rim_halo,
     send,
     recv,
     inv,
@@ -42,6 +45,7 @@
     depth_recv,
     colour_send,
     colour_recv,
+    known,
 ):
     gx, gy, me = lax.axis_index("gx"), lax.axis_index("gy"), lax.axis_index("gz")
     n_x, n_y = lax.axis_size("gx"), lax.axis_size("gy")
@@ -59,20 +63,22 @@
     ]
     below, above = {"gz": step(me, n_z, -1)}, {"gz": step(me, n_z, 1)}
 
+    reach = n_z // 4
     barrier = pltpu.get_barrier_semaphore()
+
+    def greet(by, carry):
+        for sign in (-1, 1):
+            pl.semaphore_signal(
+                barrier,
+                inc=1,
+                device_id={"gz": lax.rem(me + sign * (reach - by) + n_z, n_z)},
+                device_id_type=MESH,
+            )
+        return carry
+
+    lax.fori_loop(0, reach, greet, 0)
     for other in neighbours:
         pl.semaphore_signal(barrier, inc=1, device_id=other, device_id_type=MESH)
-
-    def greet(by, carry):
-        pl.semaphore_signal(
-            barrier,
-            inc=1,
-            device_id={"gz": lax.rem(me + by, n_z)},
-            device_id_type=MESH,
-        )
-        return carry
-
-    lax.fori_loop(1, n_z, greet, 0)
 
     loads = []
     for half in range(2):
@@ -196,53 +202,82 @@
             device_id_type=MESH,
         )
 
-    own_rows = pl.ds(ROWS, height)
-    own_planes = pl.ds(1, depth)
-    z_up = remote(
-        dens.at[depth, :, own_rows, :], dens.at[0, :, own_rows, :], 0, above
-    )
-    z_down = remote(
-        dens.at[1, :, own_rows, :],
-        dens.at[depth + 1, :, own_rows, :],
-        1,
-        below,
-    )
-    x_up = remote(
-        dens.at[own_planes, :, pl.ds(height, ROWS), :],
-        dens.at[own_planes, :, pl.ds(0, ROWS), :],
-        2,
-        neighbours[1],
-    )
-    x_down = remote(
-        dens.at[own_planes, :, pl.ds(ROWS, ROWS), :],
-        dens.at[own_planes, :, pl.ds(height + ROWS, ROWS), :],
-        3,
-        neighbours[0],
-    )
-
-    y_up = remote(edge.at[1], halo.at[0], 4, neighbours[3])
-    y_down = remote(edge.at[0], halo.at[1], 5, neighbours[2])
-    pl.semaphore_wait(barrier, len(neighbours) + n_z - 1)
-    copies = [z_up, z_down, y_up, y_down, x_up, x_down]
+    piece = height // PARTS
+
+    def z_up(part):
+        rows = pl.ds(pl.multiple_of(ROWS + part * piece, ROWS), piece)
+        return remote(
+            dens.at[depth, :, rows, :], dens.at[0, :, rows, :], 4 + part, above
+        )
+
+    def z_down(part):
+        rows = pl.ds(pl.multiple_of(ROWS + part * piece, ROWS), piece)
+        return remote(
+            dens.at[1, :, rows, :],
+            dens.at[depth + 1, :, rows, :],
+            4 + PARTS + part,
+            below,
+        )
+
+    for half in range(2):
+        top = jnp.zeros((ROWS, LANES), F32)
+        bottom = jnp.zeros((ROWS, LANES), F32)
+        for z in range(depth):
+            row = dens[z + 1, half, pl.ds(ROWS, 1), :]
+            top = jnp.where(sub == z, jnp.broadcast_to(row, top.shape), top)
+            row = dens[z + 1, half, pl.ds(height + ROWS - 1, 1), :]
+            bottom = jnp.where(sub == z, jnp.broadcast_to(row, top.shape), bottom)
+        rim[0, half] = top
+        rim[1, half] = bottom
+    x_up = remote(rim.at[1], rim_halo.at[0], 2, neighbours[1])
+    x_down = remote(rim.at[0], rim_halo.at[1], 3, neighbours[0])
+
+    @pl.when(me == 0)
+    def _():
+        for half in range(2):
+            dens[0, half, pl.ds(ROWS, height), :] = jnp.zeros((height, LANES), F32)
+
+    @pl.when(me == n_z - 1)
+    def _():
+        for half in range(2):
+            dens[depth + 1, half, pl.ds(ROWS, height), :] = jnp.zeros(
+                (height, LANES), F32
+            )
+
+    y_up = remote(edge.at[1], halo.at[0], 0, neighbours[3])
+    y_down = remote(edge.at[0], halo.at[1], 1, neighbours[2])
+    pl.semaphore_wait(barrier, len(neighbours) + 2 * reach)
+    copies = [y_up, y_down, x_up, x_down]
     for copy in copies:
         copy.start()
 
+    @pl.when(me != n_z - 1)
+    def _():
+        for part in range(PARTS):
+            z_up(part).start()
+
+    @pl.when(me != 0)
+    def _():
+        for part in range(PARTS):
+            z_down(part).start()
+
+    for sign in (-1, 1):
+        pl.semaphore_signal(
+            known,
+            inc=1,
+            device_id={"gz": step(me, n_z, sign * reach)},
+            device_id_type=MESH,
+        )
+
     def send_depth(by, carry):
-        depth_to(lax.rem(me + by, n_z)).start()
-        return carry
-
-    lax.fori_loop(1, n_z, send_depth, 0)
-    loads[6].wait()
-
-    def place(rank, carry):
-        slot = jnp.int32(0)
-        for b in range(n_z):
-            here = lax.rem(me + (n_z - b), n_z)
-            slot = jnp.where(order_ref[0, 0, b] == rank, here, slot)
-        inv[rank] = slot
-        return carry
-
-    lax.fori_loop(0, n_z, place, 0)
+        for sign in (-1, 1):
+            depth_to(lax.rem(me + sign * by + n_z, n_z)).start()
+        return carry
+
+    lax.fori_loop(1, reach + 1, send_depth, 0)
+    pl.semaphore_wait(known, 2)
+    lax.fori_loop(reach + 1, n_z // 2, send_depth, 0)
+    depth_to(lax.rem(me + n_z // 2, n_z)).start()
 
     for copy in copies:
         copy.wait_recv()
@@ -251,36 +286,41 @@
 
     @pl.when(gx == 0)
     def _():
+        for half in range(2):
+            rim_halo[0, half] = blank
+
+    @pl.when(gx == n_x - 1)
+    def _():
+        for half in range(2):
+            rim_halo[1, half] = blank
+
+    @pl.when(gy == 0)
+    def _():
+        halo[0] = blank
+
+    @pl.when(gy == n_y - 1)
+    def _():
+        halo[1] = blank
+
+    for half in range(2):
+        before, after = rim_halo[0, half], rim_halo[1, half]
         for z in range(depth):
-            for half in range(2):
-                dens[z + 1, half, pl.ds(0, ROWS), :] = blank
-
-    @pl.when(gx == n_x - 1)
-    def _():
-        for z in range(depth):
-            for half in range(2):
-                dens[z + 1, half, pl.ds(height + ROWS, ROWS), :] = blank
-
-    @pl.when(gy == 0)
-    def _():
-        halo[0] = blank
-
-    @pl.when(gy == n_y - 1)
-    def _():
-        halo[1] = blank
-
-    @pl.when(me == 0)
-    def _():
-        for half in range(2):
-            dens[0, half, own_rows, :] = jnp.zeros((height, LANES), F32)
-
-    @pl.when(me == n_z - 1)
-    def _():
-        for half in range(2):
-            dens[depth + 1, half, own_rows, :] = jnp.zeros((height, LANES), F32)
-
-    def colours(k, carry):
-        block = k
+            dens[z + 1, half, pl.ds(ROWS - 1, 1), :] = before[z : z + 1, :]
+            dens[z + 1, half, pl.ds(height + ROWS, 1), :] = after[z : z + 1, :]
+
+    def colours(block, carry):
+        part = lax.div(block * PARTS, blocks)
+
+        @pl.when(lax.rem(block * PARTS, blocks) == 0)
+        def _():
+            @pl.when(me != 0)
+            def _():
+                z_up(part).wait_recv()
+
+            @pl.when(me != n_z - 1)
+            def _():
+                z_down(part).wait_recv()
+
         rows = pl.ds(pl.multiple_of(block * ROWS, ROWS), ROWS)
         base = block * ROWS
         here = pl.ds(pl.multiple_of(base + ROWS, ROWS), ROWS)
@@ -329,6 +369,18 @@
 
     lax.fori_loop(0, blocks, colours, 0)
 
+    loads[6].wait()
+
+    def place(rank, carry):
+        slot = jnp.int32(0)
+        for b in range(n_z):
+            here = lax.rem(me + (n_z - b), n_z)
+            slot = jnp.where(order_ref[0, 0, b] == rank, here, slot)
+        inv[rank] = slot
+        return carry
+
+    lax.fori_loop(0, n_z, place, 0)
+
     recv[0] = send[me]
 
     def arrive(by, carry):
@@ -355,6 +407,17 @@
     for copy in copies:
         copy.wait_send()
 
+    @pl.when(me != n_z - 1)
+    def _():
+        for part in range(PARTS):
+            z_up(part).wait_send()
+
+    @pl.when(me != 0)
+    def _():
+        for part in range(PARTS):
+            z_down(part).wait_send()
+
+
     def leave(by, carry):
         other = lax.rem(me + by, n_z)
         depth_to(other).wait_send()
@@ -372,7 +435,7 @@
     anywhere = pl.BlockSpec(memory_space=pl.ANY)
     return pl.pallas_call(
         functools.partial(kernel, n_z, scale),
-        out_shape=jax.ShapeDtypeStruct((4, height // n_z, width), F32),
+        out_shape=pltpu.VMEM((4, height // n_z, width), F32),
         in_specs=[anywhere] * 5,
         out_specs=vmem,
         scratch_shapes=[
@@ -385,16 +448,19 @@
             pltpu.VMEM((depth, 2, height, LANES), F32),
             pltpu.VMEM((2, ROWS, LANES), F32),
             pltpu.VMEM((2, ROWS, LANES), F32),
+            pltpu.VMEM((2, 2, ROWS, LANES), F32),
+            pltpu.VMEM((2, 2, ROWS, LANES), F32),
             pltpu.VMEM((n_z, 4, ROWS, LANES), F32),
             pltpu.VMEM((n_z, 4, ROWS, LANES), F32),
             pltpu.SMEM((n_z,), jnp.int32),
             pltpu.SemaphoreType.DMA((7,)),
-            pltpu.SemaphoreType.DMA((6,)),
-            pltpu.SemaphoreType.DMA((6,)),
+            pltpu.SemaphoreType.DMA((4 + 2 * PARTS,)),
+            pltpu.SemaphoreType.DMA((4 + 2 * PARTS,)),
             pltpu.SemaphoreType.DMA((n_z,)),
             pltpu.SemaphoreType.DMA((n_z,)),
             pltpu.SemaphoreType.DMA((n_z,)),
             pltpu.SemaphoreType.DMA((n_z,)),
+            pltpu.SemaphoreType.REGULAR,
         ],
         compiler_params=pltpu.CompilerParams(collective_id=0, has_side_effects=True),
     )(density, bins, colour_table, opacity_table, order)

time: 32 us -> 30.4 us (0.950)
  the two profiles are of different devices: /device:TPU:2 before, /device:TPU:128 now
where the time goes in v3:
time: 30.4 us; the launch traced here: 30.1 us
  Pallas kernels  29.5 us (97%)
  local copies, waits for them, and re-layouts  0.61 us (2%)
    pallas_call x1, Pallas kernels, local(): pl.pallas_call(functools.partial(kernel, n_z, scale), out_shape=pltpu.VME...  29.5 us

profile of v3, /device:TPU:128, one launch (start us, length us, event | category | flops | bytes accessed | tf_op | source)
XLA Modules:
  0.0 30.1 jit_solution(9003193211174246016)
XLA Ops:
  0.0 29.5 %shard_map.55 = f32[4,4,256]{2,1,0:T(4,128)S(1)} custom-call(f32[8,64,256]{2,1,0:T(8,128)} %dens_hbm.1, s32[8,64,256]{2,1,0:T(8,128)} %bins_hbm.1, bf16[3,256]{1,0:T(4,128)(2,1)} %ctab_hbm.1, bf16[256]{0:T(256)(128)(2,1)} %otab_hbm.1, s32[1,1,16]{2,1,0:T(1,128)} %order_hbm.1), custom_call_target="tpu_custom_call" | custom-call | tf_op jit(solution)/shard_map/pallas_call | solution.py:436
  29.5 0.6 %copy.7 = f32[4,4,256]{2,1,0:T(4,128)} copy(f32[4,4,256]{2,1,0:T(4,128)S(1)} %shard_map.55) | data formatting | bytes 32768

commit v4 on v3

--- a/solution.py
+++ b/solution.py
@@ -11,7 +11,6 @@
 MESH = pl.DeviceIdType.MESH
 LANES = 128
 ROWS = 8
-PARTS = 4
 F32 = jnp.float32
 
 
@@ -175,8 +174,8 @@
         return pltpu.make_async_remote_copy(
             src_ref=send.at[other, 3],
             dst_ref=recv.at[slot, 3],
-            send_sem=depth_send.at[slot],
-            recv_sem=depth_recv.at[slot],
+            send_sem=depth_send,
+            recv_sem=depth_recv,
             device_id={"gz": other},
             device_id_type=MESH,
         )
@@ -186,8 +185,8 @@
         return pltpu.make_async_remote_copy(
             src_ref=send.at[other, pl.ds(0, 3)],
             dst_ref=recv.at[slot, pl.ds(0, 3)],
-            send_sem=colour_send.at[slot],
-            recv_sem=colour_recv.at[slot],
+            send_sem=colour_send,
+            recv_sem=colour_recv,
             device_id={"gz": other},
             device_id_type=MESH,
         )
@@ -202,22 +201,9 @@
             device_id_type=MESH,
         )
 
-    piece = height // PARTS
-
-    def z_up(part):
-        rows = pl.ds(pl.multiple_of(ROWS + part * piece, ROWS), piece)
-        return remote(
-            dens.at[depth, :, rows, :], dens.at[0, :, rows, :], 4 + part, above
-        )
-
-    def z_down(part):
-        rows = pl.ds(pl.multiple_of(ROWS + part * piece, ROWS), piece)
-        return remote(
-            dens.at[1, :, rows, :],
-            dens.at[depth + 1, :, rows, :],
-            4 + PARTS + part,
-            below,
-        )
+    rows = pl.ds(ROWS, height)
+    z_up = remote(dens.at[depth, :, rows, :], dens.at[0, :, rows, :], 4, above)
+    z_down = remote(dens.at[1, :, rows, :], dens.at[depth + 1, :, rows, :], 5, below)
 
     for half in range(2):
         top = jnp.zeros((ROWS, LANES), F32)
@@ -247,19 +233,16 @@
     y_up = remote(edge.at[1], halo.at[0], 0, neighbours[3])
     y_down = remote(edge.at[0], halo.at[1], 1, neighbours[2])
     pl.semaphore_wait(barrier, len(neighbours) + 2 * reach)
-    copies = [y_up, y_down, x_up, x_down]
-    for copy in copies:
-        copy.start()
-
-    @pl.when(me != n_z - 1)
-    def _():
-        for part in range(PARTS):
-            z_up(part).start()
-
-    @pl.when(me != 0)
-    def _():
-        for part in range(PARTS):
-            z_down(part).start()
+    has_before = (gy > 0, gx > 0, me > 0)
+    has_after = (gy < n_y - 1, gx < n_x - 1, me < n_z - 1)
+    upward, downward = (y_up, x_up, z_up), (y_down, x_down, z_down)
+
+    def sides(act, towards):
+        for copies, there in zip((upward, downward), towards):
+            for copy, here in zip(copies, there):
+                pl.when(here)(functools.partial(act, copy))
+
+    sides(lambda copy: copy.start(), (has_after, has_before))
 
     for sign in (-1, 1):
         pl.semaphore_signal(
@@ -279,8 +262,7 @@
     lax.fori_loop(reach + 1, n_z // 2, send_depth, 0)
     depth_to(lax.rem(me + n_z // 2, n_z)).start()
 
-    for copy in copies:
-        copy.wait_recv()
+    sides(lambda copy: copy.wait_recv(), (has_before, has_after))
 
     blank = jnp.zeros((ROWS, LANES), F32)
 
@@ -308,19 +290,8 @@
             dens[z + 1, half, pl.ds(ROWS - 1, 1), :] = before[z : z + 1, :]
             dens[z + 1, half, pl.ds(height + ROWS, 1), :] = after[z : z + 1, :]
 
-    def colours(block, carry):
-        part = lax.div(block * PARTS, blocks)
-
-        @pl.when(lax.rem(block * PARTS, blocks) == 0)
-        def _():
-            @pl.when(me != 0)
-            def _():
-                z_up(part).wait_recv()
-
-            @pl.when(me != n_z - 1)
-            def _():
-                z_down(part).wait_recv()
-
+    def colours(k, carry):
+        block = jnp.where(me < n_z // 2, jnp.where(k < 2, k, jnp.where(k < 6, k + 2, k - 4)), k)
         rows = pl.ds(pl.multiple_of(block * ROWS, ROWS), ROWS)
         base = block * ROWS
         here = pl.ds(pl.multiple_of(base + ROWS, ROWS), ROWS)
@@ -383,13 +354,22 @@
 
     recv[0] = send[me]
 
-    def arrive(by, carry):
-        other = lax.rem(me + by, n_z)
-        depth_to(other).wait_recv()
-        colour_to(other).wait_recv()
-        return carry
-
-    lax.fori_loop(1, n_z, arrive, 0)
+    others = pl.ds(1, n_z - 1)
+
+    def all_tiles(channels, send_sem, recv_sem):
+        return pltpu.make_async_remote_copy(
+            src_ref=send.at[others, channels],
+            dst_ref=recv.at[others, channels],
+            send_sem=send_sem,
+            recv_sem=recv_sem,
+            device_id=above,
+            device_id_type=MESH,
+        )
+
+    all_depths = all_tiles(3, depth_send, depth_recv)
+    all_colours = all_tiles(pl.ds(0, 3), colour_send, colour_recv)
+    all_depths.wait_recv()
+    all_colours.wait_recv()
 
     ahead = jnp.zeros((ROWS, LANES), F32)
     image = [jnp.zeros((ROWS, LANES), F32) for _ in range(3)]
@@ -404,27 +384,10 @@
         out_ref[c, :, 0:LANES] = image[c][0:4, :]
         out_ref[c, :, LANES : 2 * LANES] = image[c][4:8, :]
 
-    for copy in copies:
-        copy.wait_send()
-
-    @pl.when(me != n_z - 1)
-    def _():
-        for part in range(PARTS):
-            z_up(part).wait_send()
-
-    @pl.when(me != 0)
-    def _():
-        for part in range(PARTS):
-            z_down(part).wait_send()
-
-
-    def leave(by, carry):
-        other = lax.rem(me + by, n_z)
-        depth_to(other).wait_send()
-        colour_to(other).wait_send()
-        return carry
-
-    lax.fori_loop(1, n_z, leave, 0)
+    sides(lambda copy: copy.wait_send(), (has_after, has_before))
+
+    all_depths.wait_send()
+    all_colours.wait_send()
 
 
 def local(density, bins, colour_table, opacity_table, order):
@@ -454,12 +417,12 @@
             pltpu.VMEM((n_z, 4, ROWS, LANES), F32),
             pltpu.SMEM((n_z,), jnp.int32),
             pltpu.SemaphoreType.DMA((7,)),
-            pltpu.SemaphoreType.DMA((4 + 2 * PARTS,)),
-            pltpu.SemaphoreType.DMA((4 + 2 * PARTS,)),
-            pltpu.SemaphoreType.DMA((n_z,)),
-            pltpu.SemaphoreType.DMA((n_z,)),
-            pltpu.SemaphoreType.DMA((n_z,)),
-            pltpu.SemaphoreType.DMA((n_z,)),
+            pltpu.SemaphoreType.DMA((6,)),
+            pltpu.SemaphoreType.DMA((6,)),
+            pltpu.SemaphoreType.DMA,
+            pltpu.SemaphoreType.DMA,
+            pltpu.SemaphoreType.DMA,
+            pltpu.SemaphoreType.DMA,
             pltpu.SemaphoreType.REGULAR,
         ],
         compiler_params=pltpu.CompilerParams(collective_id=0, has_side_effects=True),

time: 30.4 us -> 29.1 us (0.957)
  Pallas kernels: 29.5 us -> 28.4 us
    pallas_call x1, Pallas kernels: 29.5 us -> 28.4 us  [local(): pl.pallas_call(functools.partial(kernel, n_z, scale), out_shape=pltpu.VME...]
where the time goes in v4:
time: 29.1 us; the launch traced here: 29 us
  Pallas kernels  28.4 us (98%)
  local copies, waits for them, and re-layouts  0.61 us (2%)
    pallas_call x1, Pallas kernels, local(): pl.pallas_call(functools.partial(kernel, n_z, scale), out_shape=pltpu.VME...  28.4 us
    unnamed x1, local copies, waits for them, and re-layouts  0.61 us

profile of v4, /device:TPU:128, one launch (start us, length us, event | category | flops | bytes accessed | tf_op | source)
XLA Modules:
  0.0 29.0 jit_solution(13087514531853924590)
XLA Ops:
  0.0 28.4 %shard_map.55 = f32[4,4,256]{2,1,0:T(4,128)S(1)} custom-call(f32[8,64,256]{2,1,0:T(8,128)} %dens_hbm.1, s32[8,64,256]{2,1,0:T(8,128)} %bins_hbm.1, bf16[3,256]{1,0:T(4,128)(2,1)} %ctab_hbm.1, bf16[256]{0:T(256)(128)(2,1)} %otab_hbm.1, s32[1,1,16]{2,1,0:T(1,128)} %order_hbm.1), custom_call_target="tpu_custom_call" | custom-call | tf_op jit(solution)/shard_map/pallas_call | solution.py:399
  28.4 0.6 %copy.7 = f32[4,4,256]{2,1,0:T(4,128)} copy(f32[4,4,256]{2,1,0:T(4,128)S(1)} %shard_map.55) | data formatting | bytes 32768

commit v5 on v4

--- a/solution.py
+++ b/solution.py
@@ -30,6 +30,7 @@
     order_ref,
     tabs,
     weight,
+    tinted,
     edge,
     halo,
     rim,
@@ -258,6 +259,19 @@
         return carry
 
     lax.fori_loop(1, reach + 1, send_depth, 0)
+    def tint(block, carry):
+        rows = pl.ds(pl.multiple_of(block * ROWS, ROWS), ROWS)
+        for z in range(depth):
+            for half in range(2):
+                bin_ = bins[z, half, rows, :]
+                index, upper = bin_ & (LANES - 1), bin_ >= LANES
+                for c in range(3):
+                    tinted[c, z, half, rows, :] = weight[z, half, rows, :] * looked(
+                        c, index, upper
+                    )
+        return carry
+
+    lax.fori_loop(0, blocks, tint, 0)
     pl.semaphore_wait(known, 2)
     lax.fori_loop(reach + 1, n_z // 2, send_depth, 0)
     depth_to(lax.rem(me + n_z // 2, n_z)).start()
@@ -291,7 +305,7 @@
             dens[z + 1, half, pl.ds(height + ROWS, 1), :] = after[z : z + 1, :]
 
     def colours(k, carry):
-        block = jnp.where(me < n_z // 2, jnp.where(k < 2, k, jnp.where(k < 6, k + 2, k - 4)), k)
+        block = jnp.where(me < n_z // 2, jnp.where(k < 2, k, jnp.where(k < 6, k + 2, k - 4)), jnp.where(me < n_z - n_z // 4, jnp.where(k < 2, k, jnp.where(k < 6, k + 2, k - 4)), k))
         rows = pl.ds(pl.multiple_of(block * ROWS, ROWS), ROWS)
         base = block * ROWS
         here = pl.ds(pl.multiple_of(base + ROWS, ROWS), ROWS)
@@ -322,11 +336,8 @@
                     slope_z * slope_z + slope_x * slope_x + slope_y * slope_y + 4.0
                 )
                 shade = 0.25 + facing * lax.rsqrt(square)
-                shaded = weight[z, half, rows, :] * shade
-                bin_ = bins[z, half, rows, :]
-                index, upper = bin_ & (LANES - 1), bin_ >= LANES
                 for c in range(3):
-                    sums[c][half] = sums[c][half] + shaded * looked(c, index, upper)
+                    sums[c][half] = sums[c][half] + shade * tinted[c, z, half, rows, :]
         for c in range(3):
             split(block, c, *sums[c])
 
@@ -409,6 +420,7 @@
             pltpu.SMEM(order.shape, order.dtype),
             pltpu.VMEM((4, 2, ROWS, LANES), F32),
             pltpu.VMEM((depth, 2, height, LANES), F32),
+            pltpu.VMEM((3, depth, 2, height, LANES), F32),
             pltpu.VMEM((2, ROWS, LANES), F32),
             pltpu.VMEM((2, ROWS, LANES), F32),
             pltpu.VMEM((2, 2, ROWS, LANES), F32),

time: 29.1 us -> 29.1 us (level)
  no operation moved by 1% of the time
where the time goes in v5:
time: 29.1 us; the launch traced here: 29 us
  Pallas kernels  28.4 us (98%)
  local copies, waits for them, and re-layouts  0.61 us (2%)
    pallas_call x1, Pallas kernels, local(): pl.pallas_call(functools.partial(kernel, n_z, scale), out_shape=pltpu.VME...  28.4 us
    unnamed x1, local copies, waits for them, and re-layouts  0.61 us

profile of v5, /device:TPU:128, one launch (start us, length us, event | category | flops | bytes accessed | tf_op | source)
XLA Modules:
  0.0 29.0 jit_solution(3013909579342758126)
XLA Ops:
  0.0 28.4 %shard_map.55 = f32[4,4,256]{2,1,0:T(4,128)S(1)} custom-call(f32[8,64,256]{2,1,0:T(8,128)} %dens_hbm.1, s32[8,64,256]{2,1,0:T(8,128)} %bins_hbm.1, bf16[3,256]{1,0:T(4,128)(2,1)} %ctab_hbm.1, bf16[256]{0:T(256)(128)(2,1)} %otab_hbm.1, s32[1,1,16]{2,1,0:T(1,128)} %order_hbm.1), custom_call_target="tpu_custom_call" | custom-call | tf_op jit(solution)/shard_map/pallas_call | solution.py:410
  28.4 0.6 %copy.7 = f32[4,4,256]{2,1,0:T(4,128)} copy(f32[4,4,256]{2,1,0:T(4,128)S(1)} %shard_map.55) | data formatting | bytes 32768

commit v6 on v5

--- a/solution.py
+++ b/solution.py
@@ -87,20 +87,20 @@
             pltpu.make_async_copy(
                 dens_hbm.at[:, :, lanes],
                 dens.at[pl.ds(1, depth), half, pl.ds(ROWS, height), :],
-                load_sem.at[half],
+                load_sem.at[0],
             )
         )
     for half in range(2):
         lanes = pl.ds(half * LANES, LANES)
         loads.append(
             pltpu.make_async_copy(
-                bins_hbm.at[:, :, lanes], bins.at[:, half], load_sem.at[2 + half]
+                bins_hbm.at[:, :, lanes], bins.at[:, half], load_sem.at[1]
             )
         )
     for index, (src, dst) in enumerate(
         ((ctab_hbm, ctab_ref), (otab_hbm, otab_ref), (order_hbm, order_ref))
     ):
-        loads.append(pltpu.make_async_copy(src, dst, load_sem.at[4 + index]))
+        loads.append(pltpu.make_async_copy(src, dst, load_sem.at[2 + index]))
     for load in loads:
         load.start()
     loads[4].wait()
@@ -114,8 +114,8 @@
             row = table[c : c + 1, half * LANES : (half + 1) * LANES]
             tabs[c, half] = jnp.broadcast_to(row, (ROWS, LANES))
 
-    loads[0].wait()
-    loads[1].wait()
+    own = dens.at[pl.ds(1, depth), :, pl.ds(ROWS, height), :]
+    pltpu.make_async_copy(own, own, load_sem.at[0]).wait()
 
     lane = lax.broadcasted_iota(jnp.int32, (ROWS, LANES), 1)
     sub = lax.broadcasted_iota(jnp.int32, (ROWS, LANES), 0)
@@ -147,8 +147,7 @@
             jnp.take_along_axis(tabs[c, 0], index, axis=1, mode="promise_in_bounds"),
         )
 
-    loads[2].wait()
-    loads[3].wait()
+    pltpu.make_async_copy(bins, bins, load_sem.at[1]).wait()
 
     def optical(block, carry):
         rows = pl.ds(pl.multiple_of(block * ROWS, ROWS), ROWS)
@@ -243,8 +242,6 @@
             for copy, here in zip(copies, there):
                 pl.when(here)(functools.partial(act, copy))
 
-    sides(lambda copy: copy.start(), (has_after, has_before))
-
     for sign in (-1, 1):
         pl.semaphore_signal(
             known,
@@ -252,6 +249,8 @@
             device_id={"gz": step(me, n_z, sign * reach)},
             device_id_type=MESH,
         )
+
+    sides(lambda copy: copy.start(), (has_after, has_before))
 
     def send_depth(by, carry):
         for sign in (-1, 1):
@@ -428,7 +427,7 @@
             pltpu.VMEM((n_z, 4, ROWS, LANES), F32),
             pltpu.VMEM((n_z, 4, ROWS, LANES), F32),
             pltpu.SMEM((n_z,), jnp.int32),
-            pltpu.SemaphoreType.DMA((7,)),
+            pltpu.SemaphoreType.DMA((5,)),
             pltpu.SemaphoreType.DMA((6,)),
             pltpu.SemaphoreType.DMA((6,)),
             pltpu.SemaphoreType.DMA,

time: 29.1 us -> 29.1 us (level)
  no operation moved by 1% of the time
where the time goes in v6:
time: 29.1 us; the launch traced here: 29 us
  Pallas kernels  28.3 us (97%)
  local copies, waits for them, and re-layouts  0.61 us (2%)
    pallas_call x1, Pallas kernels, local(): pl.pallas_call(functools.partial(kernel, n_z, scale), out_shape=pltpu.VME...  28.3 us
    unnamed x1, local copies, waits for them, and re-layouts  0.61 us

profile of v6, /device:TPU:128, one launch (start us, length us, event | category | flops | bytes accessed | tf_op | source)
XLA Modules:
  0.0 29.0 jit_solution(5336820983045161091)
XLA Ops:
  0.0 28.3 %shard_map.55 = f32[4,4,256]{2,1,0:T(4,128)S(1)} custom-call(f32[8,64,256]{2,1,0:T(8,128)} %dens_hbm.1, s32[8,64,256]{2,1,0:T(8,128)} %bins_hbm.1, bf16[3,256]{1,0:T(4,128)(2,1)} %ctab_hbm.1, bf16[256]{0:T(256)(128)(2,1)} %otab_hbm.1, s32[1,1,16]{2,1,0:T(1,128)} %order_hbm.1), custom_call_target="tpu_custom_call" | custom-call | tf_op jit(solution)/shard_map/pallas_call | solution.py:409
  28.4 0.6 %copy.7 = f32[4,4,256]{2,1,0:T(4,128)} copy(f32[4,4,256]{2,1,0:T(4,128)S(1)} %shard_map.55) | data formatting | bytes 32768

commit v7 on v5

--- a/solution.py
+++ b/solution.py
@@ -305,7 +305,7 @@
             dens[z + 1, half, pl.ds(height + ROWS, 1), :] = after[z : z + 1, :]
 
     def colours(k, carry):
-        block = jnp.where(me < n_z // 2, jnp.where(k < 2, k, jnp.where(k < 6, k + 2, k - 4)), jnp.where(me < n_z - n_z // 4, jnp.where(k < 2, k, jnp.where(k < 6, k + 2, k - 4)), k))
+        block = jnp.where(me < n_z // 2, jnp.where(k < 2, k, jnp.where(k < 6, k + 2, k - 4)), jnp.where(me < n_z - n_z // 4, jnp.where(k < 2, k, jnp.where(k < 6, k + 2, k - 4)), jnp.where(k < 4, k, 11 - k)))
         rows = pl.ds(pl.multiple_of(block * ROWS, ROWS), ROWS)
         base = block * ROWS
         here = pl.ds(pl.multiple_of(base + ROWS, ROWS), ROWS)

time: 29.1 us -> 29.1 us (level)
  no operation moved by 1% of the time
where the time goes in v7:
time: 29.1 us; the launch traced here: 29 us
  Pallas kernels  28.4 us (98%)
  local copies, waits for them, and re-layouts  0.61 us (2%)
    pallas_call x1, Pallas kernels, local(): pl.pallas_call(functools.partial(kernel, n_z, scale), out_shape=pltpu.VME...  28.4 us
    unnamed x1, local copies, waits for them, and re-layouts  0.61 us

profile of v7, /device:TPU:128, one launch (start us, length us, event | category | flops | bytes accessed | tf_op | source)
XLA Modules:
  0.0 29.0 jit_solution(17972754849044752472)
XLA Ops:
  0.0 28.4 %shard_map.55 = f32[4,4,256]{2,1,0:T(4,128)S(1)} custom-call(f32[8,64,256]{2,1,0:T(8,128)} %dens_hbm.1, s32[8,64,256]{2,1,0:T(8,128)} %bins_hbm.1, bf16[3,256]{1,0:T(4,128)(2,1)} %ctab_hbm.1, bf16[256]{0:T(256)(128)(2,1)} %otab_hbm.1, s32[1,1,16]{2,1,0:T(1,128)} %order_hbm.1), custom_call_target="tpu_custom_call" | custom-call | tf_op jit(solution)/shard_map/pallas_call | solution.py:410
  28.4 0.6 %copy.7 = f32[4,4,256]{2,1,0:T(4,128)} copy(f32[4,4,256]{2,1,0:T(4,128)S(1)} %shard_map.55) | data formatting | bytes 32768
